TPU v7x, 32 devices: a whole 2x2x4 slice. The times are simulated.
32 devices in a mesh: groups: 2 (over y), expert: 4 (over x, core), replica: 4 (over z).
Axes of the slice: x: 2, y: 2, z: 4, core: 2. Of those that a mesh axis runs over, the one named last changes fastest.
Arguments:
- tokens: bfloat16 [8192, 2048], P(('groups', 'expert', 'replica')), parts along dimension 0, may hold values from -6 to 6
- norm_gain: float32 [2048], replicated, may hold values from 0.1 to 1.9
- router: bfloat16 [2048, 16], replicated, may hold values from -0.125 to 0.125
- down_proj: bfloat16 [2048, 512], P(('expert', 'replica')), may hold values from -0.125 to 0.125
- up_proj: bfloat16 [2048, 512], P(('expert', 'replica')), may hold values from -0.25 to 0.25
- expert_gate: bfloat16 [16, 512, 768], P('expert'), may hold values from -0.25 to 0.25
- expert_up: bfloat16 [16, 512, 768], P('expert'), may hold values from -0.25 to 0.25
- expert_down: bfloat16 [16, 768, 512], P('expert'), may hold values from -0.21875 to 0.21875
- expert_ids: int32 [8192, 8], P(('groups', 'expert', 'replica')), parts along dimension 0, may hold values from 0 to 15, as said below
- slot_pos: int32 [8192, 8], P(('groups', 'expert', 'replica')), parts along dimension 0, may hold values from -1 to 127, as said below
- overflow_list: int32 [32, 4, 4, 4], P(('groups', 'expert', 'replica')), parts along dimension 0, may hold values from -1 to 2047, as said below
Outputs:
- mixed: bfloat16 [8192, 2048], P(('groups', 'expert', 'replica')), parts along dimension 0
There are 2 independent parts, one for each index of `groups`. A program takes and returns all parts, laid end to end along the dimension named above; an argument that names none is the same for every part. Nothing has to cross between parts.
Inputs may be any that keep to these rules, and one draw needn't show every extreme that they name: `expert_ids`: the 8 ids of a token are distinct. `slot_pos`: within the 256 rows of one device, the choices of one expert that have a slot hold distinct slots 0, 1, 2, ... in row order, so at most 128 from one device to one expert; in every draw some expert gets all 128 slots from every device. `overflow_list`: an entry is a choice index t' * 8 + k of the source device's own rows whose expert is (destination index of the expert axis) * 4 + (local expert) and whose slot_pos is -1; each choice is listed at most once. In every draw some expert is listed at every copy by every source device.
All inputs are finite; a program needn't handle non-finite values.
Results may differ from a plain program's by a relative error of at most 0.0088.
Values may be sent and summed in bfloat16 or wider, within the bound.
A program may use at most 128 MiB of HBM per device.

v0:
```python
import jax
import jax.numpy as jnp
from jax import lax
from jax.sharding import PartitionSpec as P

epsilon = 1e-06


def run_experts(rows, w_gate, w_up, w_down):
    gate = jnp.einsum("erl,elf->erf", rows, w_gate, preferred_element_type=jnp.float32)
    upper = jnp.einsum("erl,elf->erf", rows, w_up, preferred_element_type=jnp.float32)
    hidden = (jax.nn.silu(gate) * upper).astype(jnp.bfloat16)
    return jnp.einsum("erf,efl->erl", hidden, w_down, preferred_element_type=jnp.float32).astype(
        jnp.bfloat16
    )


def on_device(
    tokens,
    norm_gain,
    router,
    down_proj,
    up_proj,
    expert_gate,
    expert_up,
    expert_down,
    expert_ids,
    slot_pos,
    overflow_list,
):
    tok_rows = tokens.shape[0]
    top_count = expert_ids.shape[1]
    local_count = expert_gate.shape[0]
    latent_width = down_proj.shape[1]
    shards = lax.axis_size("expert")
    copies = lax.axis_size("replica")
    sources = shards * copies
    capacity = tok_rows * top_count // (local_count * shards)
    row_count = shards * capacity
    spilled = local_count * row_count
    down_full, up_full = (
        lax.all_gather(down_proj, ("expert", "replica"), axis=0, tiled=True),
        lax.all_gather(up_proj, ("expert", "replica"), axis=0, tiled=True),
    )
    values = tokens.astype(jnp.float32)
    scaled = values * lax.rsqrt(jnp.mean(values * values, axis=-1, keepdims=True) + epsilon)
    normed = (scaled * norm_gain).astype(jnp.bfloat16)
    latent = jnp.dot(normed, down_full, preferred_element_type=jnp.float32).astype(jnp.bfloat16)
    logits = jnp.dot(normed, router, preferred_element_type=jnp.float32)
    chosen = jnp.take_along_axis(logits, expert_ids, axis=1)
    sigmas = jax.nn.sigmoid(chosen)
    gates = (sigmas / jnp.sum(sigmas, axis=1, keepdims=True)).reshape(-1)
    flat_ids = expert_ids.reshape(-1)
    flat_pos = slot_pos.reshape(-1)
    kept = flat_pos >= 0
    target = (
        flat_ids % local_count * row_count
        + flat_ids // local_count * capacity
        + jnp.maximum(flat_pos, 0)
    )
    repeated = jnp.repeat(latent, top_count, axis=0)
    outgoing = jnp.zeros((spilled, latent_width), jnp.bfloat16)
    outgoing = outgoing.at[jnp.where(kept, target, spilled)].set(repeated, mode="drop")
    outgoing = outgoing.reshape(local_count, row_count, latent_width)
    listed = jnp.transpose(overflow_list[0], (2, 0, 1))
    listed_safe = jnp.maximum(listed, 0)
    extra = jnp.where(
        (listed >= 0)[..., None], latent[listed_safe // top_count], jnp.zeros((), jnp.bfloat16)
    )
    first_rows = lax.all_to_all(outgoing, "expert", split_axis=1, concat_axis=1, tiled=True)
    spare_rows = lax.all_to_all(
        extra.reshape(local_count, sources, latent_width),
        ("expert", "replica"),
        split_axis=1,
        concat_axis=1,
        tiled=True,
    )
    done = run_experts(
        jnp.concatenate([first_rows, spare_rows], axis=1), expert_gate, expert_up, expert_down
    )
    spare_back = lax.all_to_all(
        done[:, row_count:], ("expert", "replica"), split_axis=1, concat_axis=1, tiled=True
    )
    returned = lax.all_to_all(
        done[:, :row_count], "expert", split_axis=1, concat_axis=1, tiled=True
    )
    returned_flat = returned.reshape(spilled, latent_width)
    picked = returned_flat[target].astype(jnp.float32)
    weight = jnp.where(kept, gates, jnp.zeros((), jnp.float32))
    combined = jnp.sum(
        (picked * weight[:, None]).reshape(tok_rows, top_count, latent_width), axis=1
    )
    listed_flat = listed.reshape(-1)
    listed_index = jnp.maximum(listed_flat, 0)
    spare_weight = jnp.where(listed_flat >= 0, gates[listed_index], jnp.zeros((), jnp.float32))
    spare_values = spare_back.reshape(-1, latent_width).astype(jnp.float32)
    combined = combined.at[listed_index // top_count].add(spare_values * spare_weight[:, None])
    merged = combined.astype(jnp.bfloat16)
    output = lax.dot_general(
        merged, up_full, (((1,), (1,)), ((), ())), preferred_element_type=jnp.float32
    )
    return output.astype(jnp.bfloat16)


def solution(mesh):
    placed = (
        P(("groups", "expert", "replica"), None),
        P(),
        P(),
        P(("expert", "replica"), None),
        P(("expert", "replica"), None),
        P("expert", None, None),
        P("expert", None, None),
        P("expert", None, None),
        P(("groups", "expert", "replica"), None),
        P(("groups", "expert", "replica"), None),
        P(("groups", "expert", "replica"), None, None, None),
    )
    return jax.shard_map(
        on_device,
        mesh=mesh,
        in_specs=placed,
        out_specs=P(("groups", "expert", "replica"), None),
        check_vma=False,
    )
```

profile of v0, /device:TPU:0, one launch (start us, length us, event | category | flops | bytes accessed | tf_op | source)
XLA Modules:
  0.0 205.2 jit_solution(5621524426477056946)
XLA Ops:
  6.5 0.0 copy-start
  6.5 0.0 all-gather.3.cloned.1.call-start
  6.5 0.7 all-gather.3.cloned.1.call-update
  7.3 1.0 copy.78
  8.3 0.7 bitcast_or_fusion
  9.0 0.1 copy.89
  9.1 0.1 reshape.362
  9.3 1.5 fusion.2
  10.8 1.7 fusion.12
  12.5 0.0 copy-start.4
  12.5 16.8 %gather_fusion.3 = f32[2048]{0:T(1024)S(1)} fusion(f32[256,16]{0,1:T(8,128)S(1)} %fusion.12, s32[2048]{0:T(1024)S(1)} %reshape.362), kind=kCustom, calls=%fused_computation.3 | custom fusion | bytes 32768 | tf_op jit(solution)/shard_map/jit(take_along_axis)/gather | solution.py:50
  29.3 0.1 reshape.365
  29.4 0.1 copy.90
  29.5 0.2 copy.77
  29.7 0.1 ge.43
  29.8 0.1 copy.79
  30.0 0.1 max.44
  30.1 0.1 reshape.323
  30.2 0.1 compare_select_fusion
  30.3 23.4 %all-gather.3.cloned.1.call-done = bf16[2048,512]{1,0:T(8,128)(2,1)} async-done(((bf16[128,512]{1,0:T(8,128)(2,1)}), bf16[2048,512]{1,0:T(8,128)(2,1)}) %all-gather.3.cloned.1.call-update) | async-done | bytes 2097168 | tf_op jit(solution)/shard_map/all_gather | solution.py:42
  53.8 2.7 %convolution_convert_fusion.1 = bf16[256,512]{1,0:T(8,128)(2,1)S(1)} fusion(bf16[2048,512]{1,0:T(8,128)(2,1)} %all-gather.3.cloned.1.call-done, bf16[256,2048]{1,0:T(8,128)(2,1)} %param.11, f32[2048]{0:T(1024)S(1)} %copy-done.4, f32[256]{0:T(256)S(1)} %add_rsqrt_fusion), kind=kOutput, calls=%fused_computation.21 | convolution fusion | flops 539099136 | bytes 3417088 | tf_op jit(solution)/shard_map/dot_general | solution.py:48
  56.4 11.0 %scatter_custom_fusion = bf16[2048,512]{1,0:T(8,128)(2,1)} fusion(s32[2048]{0:T(1024)S(1)} %bitcast.55, bf16[256,512]{1,0:T(8,128)(2,1)S(1)} %convolution_convert_fusion.1, bf16[]{:T(256)} %constant.78.clone.1), kind=kCustom, calls=%fused_computation.16 | custom fusion | bytes 2359298 | tf_op jit(solution)/shard_map/scatter | solution.py:63
  67.4 4.5 %copy.80 = bf16[4,512,512]{2,0,1:T(4,128)(2,1)} copy(bf16[4,512,512]{2,1,0:T(8,128)(2,1)} %bitcast.50) | data formatting | bytes 4194304 | tf_op jit(solution)/shard_map/reshape | solution.py:64
  72.0 4.6 %all-to-all-start = ((bf16[4,512,512]{2,0,1:T(4,128)(2,1)}), bf16[4,512,512]{2,0,1:T(4,128)(2,1)}, u32[]{:S(2)}, u32[]{:S(2)}) async-start(bf16[4,512,512]{2,0,1:T(4,128)(2,1)} %copy.80), calls=%async_computation | async-start | bytes 4194304 | tf_op jit(solution)/shard_map/all_to_all | solution.py:70
  76.6 0.0 all-gather.5.cloned.1.call-start
  76.7 0.7 all-gather.5.cloned.1.call-update
  77.4 0.1 copy.83
  77.5 0.1 reshape.340
  77.7 0.7 gather_fusion
  78.4 0.7 copy_select_fusion
  79.1 24.7 %all-to-all-done = bf16[4,512,512]{2,0,1:T(4,128)(2,1)} async-done(((bf16[4,512,512]{2,0,1:T(4,128)(2,1)}), bf16[4,512,512]{2,0,1:T(4,128)(2,1)}, u32[]{:S(2)}, u32[]{:S(2)}) %all-to-all-start) | async-done | bytes 2097184 | tf_op jit(solution)/shard_map/all_to_all | solution.py:70
  103.8 3.7 %all-to-all-start.1 = ((bf16[4,16,512]{2,0,1:T(4,128)(2,1)}), bf16[4,16,512]{2,0,1:T(4,128)(2,1)S(1)}, u32[]{:S(2)}, u32[]{:S(2)}) async-start(bf16[4,16,512]{2,0,1:T(4,128)(2,1)} %copy_select_fusion), calls=%async_computation.1 | async-start | bytes 131072 | tf_op jit(solution)/shard_map/all_to_all | solution.py:71
  107.5 3.4 %copy_dynamic-update-slice_fusion = bf16[4,528,512]{2,1,0:T(8,128)(2,1)} fusion(bf16[4,512,512]{2,0,1:T(4,128)(2,1)} %all-to-all-done), kind=kLoop, calls=%fused_computation.18 | loop fusion | bytes 4194304
  110.8 3.8 %all-to-all-done.1 = bf16[4,16,512]{2,0,1:T(4,128)(2,1)S(1)} async-done(((bf16[4,16,512]{2,0,1:T(4,128)(2,1)}), bf16[4,16,512]{2,0,1:T(4,128)(2,1)S(1)}, u32[]{:S(2)}, u32[]{:S(2)}) %all-to-all-start.1) | async-done | bytes 65568 | tf_op jit(solution)/shard_map/all_to_all | solution.py:71
  114.6 0.6 copy_dynamic-update-slice_fusion.1
  115.3 0.0 copy-done
  115.3 6.2 %fusion.26 = f32[4,528,768]{2,1,0:T(8,128)} fusion(bf16[4,528,512]{2,1,0:T(8,128)(2,1)} %copy_dynamic-update-slice_fusion.1, bf16[4,512,768]{2,1,0:T(8,128)(2,1)S(1)} %copy-done), kind=kOutput, calls=%fused_computation.69 | convolution fusion | flops 1660944384 | bytes 11796480 | tf_op jit(solution)/shard_map/erl,elf->erf/dot_general | solution.py:10
  121.5 10.6 %fusion.9 = bf16[4,528,512]{2,1,0:T(8,128)(2,1)} fusion(bf16[4,768,512]{2,1,0:T(8,128)(2,1)} %param.18, f32[4,528,768]{2,1,0:T(8,128)} %fusion.26, bf16[4,528,512]{2,1,0:T(8,128)(2,1)} %copy_dynamic-update-slice_fusion.1, bf16[4,512,768]{2,1,0:T(8,128)(2,1)} %param.17), kind=kOutput, calls=%fused_computation.20 | convolution fusion | flops 3332702208 | bytes 17104896 | tf_op jit(solution)/shard_map/erf,efl->erl/dot_general | solution.py:13
  132.0 0.8 slice.17
  132.9 0.7 copy.94
  133.6 3.5 %all-to-all-start.3 = ((bf16[4,16,512]{2,0,1:T(4,128)(2,1)}), bf16[4,16,512]{2,0,1:T(4,128)(2,1)S(1)}, u32[]{:S(2)}, u32[]{:S(2)}) async-start(bf16[4,16,512]{2,0,1:T(4,128)(2,1)} %copy.94), calls=%async_computation.3 | async-start | bytes 131072 | tf_op jit(solution)/shard_map/all_to_all | solution.py:81
  137.1 0.0 slice-start
  137.1 1.6 slice-done
  138.7 2.9 %copy.87 = bf16[4,512,512]{2,0,1:T(4,128)(2,1)} copy(bf16[4,512,512]{2,1,0:T(8,128)(2,1)S(1)} %slice-done) | data formatting | bytes 4194304 | tf_op jit(solution)/shard_map/slice | solution.py:85
  141.6 2.0 all-to-all-done.3
  143.7 4.4 %all-to-all-start.2 = ((bf16[4,512,512]{2,0,1:T(4,128)(2,1)}), bf16[4,512,512]{2,0,1:T(4,128)(2,1)}, u32[]{:S(2)}, u32[]{:S(2)}) async-start(bf16[4,512,512]{2,0,1:T(4,128)(2,1)} %copy.87), calls=%async_computation.2 | async-start | bytes 4194304 | tf_op jit(solution)/shard_map/all_to_all | solution.py:84
  148.1 0.1 copy.91
  148.2 0.1 copy.97
  148.4 0.1 reshape.336
  148.5 0.1 copy.98
  148.6 0.1 reshape.356
  148.7 0.1 copy.96
  148.8 0.1 ge.48
  148.9 0.1 copy.93
  149.1 0.1 reshape.392
  149.2 0.1 copy.92
  149.3 0.1 reshape.402
  149.4 0.8 gather_fusion.2
  150.2 23.6 %all-to-all-done.2 = bf16[4,512,512]{2,0,1:T(4,128)(2,1)} async-done(((bf16[4,512,512]{2,0,1:T(4,128)(2,1)}), bf16[4,512,512]{2,0,1:T(4,128)(2,1)}, u32[]{:S(2)}, u32[]{:S(2)}) %all-to-all-start.2) | async-done | bytes 2097184 | tf_op jit(solution)/shard_map/all_to_all | solution.py:84
  173.8 3.3 %copy.88 = bf16[4,512,512]{2,1,0:T(8,128)(2,1)} copy(bf16[4,512,512]{2,0,1:T(4,128)(2,1)} %all-to-all-done.2) | data formatting | bytes 4194304 | tf_op jit(solution)/shard_map/all_to_all | solution.py:84
  177.2 11.1 %gather_fusion.1 = bf16[2048,512]{1,0:T(8,128)(2,1)} fusion(bf16[2048,512]{1,0:T(8,128)(2,1)} %bitcast.49, s32[2048]{0:T(1024)S(1)} %broadcast_clamp_fusion), kind=kCustom, calls=%fused_computation.1 | custom fusion | bytes 4202496 | tf_op jit(solution)/shard_map/gather | solution.py:88
  188.3 3.7 %fusion = f32[256,512]{1,0:T(8,128)} fusion(bf16[2048,512]{1,0:T(8,128)(2,1)} %gather_fusion.1, f32[256,8]{1,0:T(8,128)S(1)} %copy.91), kind=kLoop, calls=%fused_computation.8 | loop fusion | flops 3014656 | bytes 2629632 | tf_op jit(solution)/shard_map/reduce_sum | solution.py:90
  192.0 2.8 %scatter_custom_fusion.1 = f32[256,512]{1,0:T(8,128)} fusion(f32[256,512]{1,0:T(8,128)} %fusion, s32[64]{0:T(128)S(1)} %fusion.23, bf16[64,512]{1,0:T(8,128)(2,1)S(1)} %bitcast.52, f32[64]{0:T(128)S(1)} %broadcast_select_fusion.1), kind=kCustom, calls=%fused_computation.27 | custom fusion | flops 98304 | bytes 590336 | tf_op jit(solution)/shard_map/scatter-add | solution.py:97
  194.8 3.5 %convolution_convert_fusion = bf16[256,2048]{1,0:T(8,128)(2,1)} fusion(bf16[2048,512]{1,0:T(8,128)(2,1)} %all-gather.5.cloned.1.call-done, f32[256,512]{1,0:T(8,128)} %scatter_custom_fusion.1), kind=kOutput, calls=%fused_computation.12 | convolution fusion | flops 537526272 | bytes 3670016 | tf_op jit(solution)/shard_map/dot_general | solution.py:99
  (24 shorter events, 0.2 us)
Async XLA Ops:
  6.5 108.8 %copy-start = (bf16[4,512,768]{2,1,0:T(8,128)(2,1)S(1)}, bf16[4,512,768]{2,1,0:T(8,128)(2,1)}, u32[]{:S(2)}) copy-start(bf16[4,512,768]{2,1,0:T(8,128)(2,1)} %param.16) | copy-start | bytes 9437188
  6.5 47.2 %all-gather.3.cloned.1.call-start = ((), (), s32[]{:S(2)}) async-start(), calls=%async_computation.4 | async-start | bytes 2228224 | tf_op jit(solution)/shard_map/all_gather | solution.py:42
  12.5 17.0 %copy-start.2 = (s32[256,8]{0,1:T(8,128)S(1)}, s32[256,8]{0,1:T(8,128)}, u32[]{:S(2)}) copy-start(s32[256,8]{0,1:T(8,128)} %param.19) | copy-start | bytes 24580
  12.5 17.0 %copy-start.3 = (s32[256,8]{0,1:T(8,128)S(1)}, s32[256,8]{0,1:T(8,128)}, u32[]{:S(2)}) copy-start(s32[256,8]{0,1:T(8,128)} %param.20) | copy-start | bytes 24580
  12.5 41.3 %copy-start.4 = (f32[2048]{0:T(1024)S(1)}, f32[2048]{0:T(1024)}, u32[]{:S(2)}) copy-start(f32[2048]{0:T(1024)} %param.12) | copy-start | bytes 24580
  72.0 5.4 %copy-start.1 = (s32[1,4,4,4]{3,2,1,0:T(4,128)S(1)}, s32[1,4,4,4]{3,2,1,0:T(4,128)}, u32[]{:S(2)}) copy-start(s32[1,4,4,4]{3,2,1,0:T(4,128)} %param.21) | copy-start | bytes 772
  72.0 31.8 %all-to-all-start = ((bf16[4,512,512]{2,0,1:T(4,128)(2,1)}), bf16[4,512,512]{2,0,1:T(4,128)(2,1)}, u32[]{:S(2)}, u32[]{:S(2)}) async-start(bf16[4,512,512]{2,0,1:T(4,128)(2,1)} %copy.80), calls=%async_computation | async-start | bytes 4194304 | tf_op jit(solution)/shard_map/all_to_all | solution.py:70
  76.6 118.2 %all-gather.5.cloned.1.call-start = ((), (), s32[]{:S(2)}) async-start(), calls=%async_computation.5 | async-start | bytes 2228224 | tf_op jit(solution)/shard_map/all_gather | solution.py:43
  103.8 10.9 %all-to-all-start.1 = ((bf16[4,16,512]{2,0,1:T(4,128)(2,1)}), bf16[4,16,512]{2,0,1:T(4,128)(2,1)S(1)}, u32[]{:S(2)}, u32[]{:S(2)}) async-start(bf16[4,16,512]{2,0,1:T(4,128)(2,1)} %copy_select_fusion), calls=%async_computation.1 | async-start | bytes 131072 | tf_op jit(solution)/shard_map/all_to_all | solution.py:71
  133.6 10.1 %all-to-all-start.3 = ((bf16[4,16,512]{2,0,1:T(4,128)(2,1)}), bf16[4,16,512]{2,0,1:T(4,128)(2,1)S(1)}, u32[]{:S(2)}, u32[]{:S(2)}) async-start(bf16[4,16,512]{2,0,1:T(4,128)(2,1)} %copy.94), calls=%async_computation.3 | async-start | bytes 131072 | tf_op jit(solution)/shard_map/all_to_all | solution.py:81
  137.1 1.6 slice-start
  143.7 30.2 %all-to-all-start.2 = ((bf16[4,512,512]{2,0,1:T(4,128)(2,1)}), bf16[4,512,512]{2,0,1:T(4,128)(2,1)}, u32[]{:S(2)}, u32[]{:S(2)}) async-start(bf16[4,512,512]{2,0,1:T(4,128)(2,1)} %copy.87), calls=%async_computation.2 | async-start | bytes 4194304 | tf_op jit(solution)/shard_map/all_to_all | solution.py:84
Sparse Core Ops, SparseCore 0:
  9.5 44.1 all-gather.2
  79.7 43.5 all-gather.4
where the time goes:
time: 206 us; the launch traced here: 205 us
  waiting for transfers between devices  78.9 us (38%)
  local copies, waits for them, and re-layouts  61.9 us (30%)
  matrix products  24.6 us (12%)
  starting transfers between devices  16.3 us (8%)
  between operations  13.7 us (7%)
  other arithmetic  9.75 us (5%)
    all_to_all x1, waiting for transfers between devices, on_device(): lax.all_to_all(outgoing, 'expert', split_axis=1, concat_axis=1, tiled=True)  24.7 us
    all_to_all x1, waiting for transfers between devices, on_device(): lax.all_to_all(done[:, :row_count], 'expert', split_axis=1, concat_axis=1...  23.6 us
    all_gather x1, waiting for transfers between devices, on_device(): lax.all_gather(down_proj, ('expert', 'replica'), axis=0, tiled=True)  23.4 us
    gather x5, local copies, waits for them, and re-layouts, on_device(): chosen = jnp.take_along_axis(logits, expert_ids, axis=1)  17.2 us
    gather x1, local copies, waits for them, and re-layouts, on_device(): picked = returned_flat[target].astype(jnp.float32)  11.1 us
    scatter x1, local copies, waits for them, and re-layouts, on_device(): outgoing.at[jnp.where(kept, target, spilled)].set(repeated, mode='drop')  11 us
    dot_general x1, matrix products, run_experts(): jnp.einsum('erf,efl->erl', hidden, w_down, preferred_element_type=jnp.flo...  10.6 us
    dot_general x1, matrix products, run_experts(): jnp.einsum('erl,elf->erf', rows, w_gate, preferred_element_type=jnp.float32)  6.18 us
  transfers between devices with their start and end apart: 6, of which 5 were waited for; matrix products, arithmetic and copies ran while one was open for 36% of the time, Pallas kernels for 0%

commit v1 on v0

v1 whole, which is shorter than its diff:
```python
import functools

import jax
import jax.numpy as jnp
from jax import lax
from jax.experimental import pallas as pl
from jax.experimental.pallas import tpu as pltpu
from jax.sharding import PartitionSpec as P

epsilon = 1e-06
CORES = 2
MESH = pl.DeviceIdType.MESH


def remote(src, dst, send, recv, where):
    return pltpu.make_async_remote_copy(
        src_ref=src, dst_ref=dst, send_sem=send, recv_sem=recv, device_id=where, device_id_type=MESH
    )


def layer(
    shards, copies, tok, gain, router, down, up, wg, wu, wd, ids, slot, ov, out,
    tokv, normed, dfull, ufull, gv, uv, dv, lat, wts, hid, acc, own, pbuf, rbuf,
    loc, dzs, dzr, dxs, dxr, dcs, dcr, uzs, uzr, uxs, uxr, ucs, ucr,
    lps, lpr, lxs, lxr, lfs, lfr, wps, wpr, wxs, wxr, wfs, wfr, rs, rr,
):
    columns = shards // CORES
    e, r = lax.axis_index("expert"), lax.axis_index("replica")
    x, c = e // CORES, e % CORES
    part = rows = down.shape[0]
    local = wg.shape[0]
    tokens = tok.shape[0]
    top = ids.shape[1]
    experts = router.shape[1]

    def ex(xx, cc):
        return xx * CORES + cc

    def back(d):
        return lax.rem(x - d + columns, columns)

    def fore(d):
        return lax.rem(x + d, columns)

    def zback(d):
        return lax.rem(r - d + copies, copies)

    def zdev(d):
        return {"replica": lax.rem(r + d, copies)}

    def xdev(d):
        return {"expert": ex(fore(d), c)}

    pdev = {"expert": ex(x, 1 - c)}

    def at(ref, index, n=1):
        return ref.at[pl.ds(pl.multiple_of(index * part, part), part * n), :]

    barrier = pltpu.get_barrier_semaphore()
    count = 1
    pl.semaphore_signal(barrier, inc=1, device_id=pdev, device_id_type=MESH)
    for d in range(1, copies):
        pl.semaphore_signal(barrier, inc=1, device_id=zdev(d), device_id_type=MESH)
        count += 1
    for d in range(1, columns):
        for cc in (c, 1 - c):
            pl.semaphore_signal(
                barrier, inc=1, device_id={"expert": ex(fore(d), cc)}, device_id_type=MESH
            )
            count += 1
    tcopy = pltpu.make_async_copy(tok, tokv, loc.at[0])
    mine = e * copies + r
    dcopy = pltpu.make_async_copy(down, at(dfull, mine), loc.at[1])
    ucopy = pltpu.make_async_copy(up, at(ufull, mine), loc.at[2])
    wcopies = [
        pltpu.make_async_copy(wg, gv, loc.at[3]),
        pltpu.make_async_copy(wu, uv, loc.at[4]),
        pltpu.make_async_copy(wd, dv, loc.at[5]),
    ]
    tcopy.start()
    dcopy.start()
    pl.semaphore_wait(barrier, count)

    sends = []

    def go(copy):
        copy.start()
        sends.append(copy)

    for d in range(1, columns):
        go(remote(down, at(dfull, mine), dxs.at[d - 1, 0], dxr.at[d - 1, 0], xdev(d)))
    for d in range(1, copies):
        go(remote(down, at(dfull, mine), dzs.at[d - 1], dzr.at[d - 1], zdev(d)))
    ucopy.start()
    for w in wcopies:
        w.start()

    tcopy.wait()
    step = 32

    @pl.loop(0, tokens // step)
    def _(i):
        at_rows = pl.ds(pl.multiple_of(i * step, step), step)
        v = tokv[at_rows, :].astype(jnp.float32)
        scaled = v * lax.rsqrt(jnp.mean(v * v, axis=-1, keepdims=True) + epsilon)
        normed[at_rows, :] = (scaled * gain[...]).astype(jnp.bfloat16)

    logits = jnp.dot(normed[...], router[...], preferred_element_type=jnp.float32)
    sig = 1.0 / (1.0 + jnp.exp(-logits))
    lane = lax.broadcasted_iota(jnp.int32, (tokens, experts), 1)
    row = lax.broadcasted_iota(jnp.int32, (tokens, experts), 0)
    chosen = jnp.zeros((tokens, experts), jnp.float32)
    served = jnp.zeros((tokens, experts), jnp.float32)
    for k in range(top):
        hit = lane == ids[:, k : k + 1]
        chosen = jnp.where(hit, 1.0, chosen)
        served = jnp.where(hit & (slot[:, k : k + 1] >= 0), 1.0, served)
    listed = jnp.concatenate([ov[0, d] for d in range(shards)], axis=1)
    for k in range(copies):
        entry = listed[k : k + 1, :]
        first = row * top
        served = jnp.where((entry >= first) & (entry < first + top), 1.0, served)
    weight = served * (sig / jnp.sum(chosen * sig, axis=1, keepdims=True))
    flipped = weight.T
    wts[e] = jnp.zeros(wts.shape[1:], jnp.float32)
    for d in range(shards):
        wts[e, d, 0:local, :] = flipped[d * local : (d + 1) * local, :]

    for j in range(1, copies):
        s = e * copies + zback(j)
        remote(down, at(dfull, s), dzs.at[j - 1], dzr.at[j - 1], zdev(j)).wait_recv()
        for d in range(1, columns):
            go(remote(at(dfull, s), at(dfull, s), dxs.at[d - 1, j], dxr.at[d - 1, j], xdev(d)))
    dcopy.wait()
    s = e * copies
    go(remote(at(dfull, s, copies), at(dfull, s, copies), dcs.at[0], dcr.at[0], pdev))
    for d in range(1, columns):
        go(remote(up, at(ufull, mine), uxs.at[d - 1], uxr.at[d - 1], xdev(d)))
    ucopy.wait()
    for z in range(1, copies):
        go(remote(at(ufull, mine), at(ufull, mine), uzs.at[z - 1, 0], uzr.at[z - 1, 0], zdev(z)))
    for d in range(1, columns):
        base = ex(back(d), c) * copies
        for j in range(copies):
            s = base + zback(j)
            remote(at(dfull, s), at(dfull, s), dxs.at[d - 1, j], dxr.at[d - 1, j], xdev(d)).wait_recv()
        go(remote(at(dfull, base, copies), at(dfull, base, copies), dcs.at[d], dcr.at[d], pdev))
    for d in range(columns):
        s = ex(back(d), 1 - c) * copies
        remote(at(dfull, s, copies), at(dfull, s, copies), dcs.at[d], dcr.at[d], pdev).wait_recv()

    lat[e] = jnp.dot(normed[...], dfull[...], preferred_element_type=jnp.float32).astype(jnp.bfloat16)
    for d in range(1, columns):
        go(remote(lat.at[e], lat.at[e], lxs.at[d - 1], lxr.at[d - 1], xdev(d)))
        go(remote(wts.at[e], wts.at[e], wxs.at[d - 1], wxr.at[d - 1], xdev(d)))
    go(remote(lat.at[e], lat.at[e], lps, lpr, pdev))
    go(remote(wts.at[e], wts.at[e], wps, wpr, pdev))

    width = wg.shape[2]
    piece = 256

    def experts_on(which):
        scale = wts[which, e].T
        spot = lax.broadcasted_iota(jnp.int32, scale.shape, 1)
        acc[...] = jnp.zeros_like(acc)

        @pl.loop(0, local)
        def _(n):
            block = lat[which]
            weights = jnp.sum(jnp.where(spot == n, scale, 0.0), axis=1, keepdims=True)
            for f in range(0, width, piece):
                a = jnp.dot(block, gv[n, :, f : f + piece], preferred_element_type=jnp.float32)
                b = jnp.dot(block, uv[n, :, f : f + piece], preferred_element_type=jnp.float32)
                h = a / (1.0 + jnp.exp(-a)) * b * weights
                hid[:, f : f + piece] = h.astype(jnp.bfloat16)
            acc[...] += jnp.dot(hid[...], dv[n], preferred_element_type=jnp.float32)

    for w in wcopies:
        w.wait()
    experts_on(e)
    own[...] = acc[...]
    for d in range(1, columns):
        s = ex(back(d), c) * copies + r
        remote(up, at(ufull, s), uxs.at[d - 1], uxr.at[d - 1], xdev(d)).wait_recv()
        for z in range(1, copies):
            go(remote(at(ufull, s), at(ufull, s), uzs.at[z - 1, d], uzr.at[z - 1, d], zdev(z)))
    p = ex(x, 1 - c)
    remote(lat.at[p], lat.at[p], lps, lpr, pdev).wait_recv()
    remote(wts.at[p], wts.at[p], wps, wpr, pdev).wait_recv()
    experts_on(p)
    pbuf[p] = acc[...].astype(jnp.bfloat16)
    go(remote(pbuf.at[p], rbuf.at[0], rs.at[0], rr.at[0], pdev))
    for d in range(1, columns):
        q = ex(back(d), c)
        remote(lat.at[q], lat.at[q], lxs.at[d - 1], lxr.at[d - 1], xdev(d)).wait_recv()
        remote(wts.at[q], wts.at[q], wxs.at[d - 1], wxr.at[d - 1], xdev(d)).wait_recv()
        go(remote(lat.at[q], lat.at[q], lfs.at[d - 1], lfr.at[d - 1], pdev))
        go(remote(wts.at[q], wts.at[q], wfs.at[d - 1], wfr.at[d - 1], pdev))
        experts_on(q)
        pbuf[q] = acc[...].astype(jnp.bfloat16)
        k = 2 * d - 1
        go(remote(pbuf.at[q], rbuf.at[k], rs.at[k], rr.at[k], {"expert": q}))
        q = ex(back(d), 1 - c)
        remote(lat.at[q], lat.at[q], lfs.at[d - 1], lfr.at[d - 1], pdev).wait_recv()
        remote(wts.at[q], wts.at[q], wfs.at[d - 1], wfr.at[d - 1], pdev).wait_recv()
        experts_on(q)
        pbuf[q] = acc[...].astype(jnp.bfloat16)
        k = 2 * d
        go(remote(pbuf.at[q], rbuf.at[k], rs.at[k], rr.at[k], {"expert": q}))

    for d in range(columns):
        base = ex(back(d), c) * copies
        for z in range(1, copies):
            s = base + zback(z)
            remote(at(ufull, s), at(ufull, s), uzs.at[z - 1, d], uzr.at[z - 1, d], zdev(z)).wait_recv()
        go(remote(at(ufull, base, copies), at(ufull, base, copies), ucs.at[d], ucr.at[d], pdev))
    for d in range(columns):
        s = ex(back(d), 1 - c) * copies
        remote(at(ufull, s, copies), at(ufull, s, copies), ucs.at[d], ucr.at[d], pdev).wait_recv()
    for k in range(shards - 1):
        remote(rbuf.at[k], rbuf.at[k], rs.at[k], rr.at[k], pdev).wait_recv()
        own[...] += rbuf[k].astype(jnp.float32)
    out[...] = lax.dot_general(
        own[...].astype(jnp.bfloat16), ufull[...], (((1,), (1,)), ((), ())),
        preferred_element_type=jnp.float32,
    ).astype(jnp.bfloat16)
    for copy in sends:
        copy.wait_send()


def on_device(
    tokens, norm_gain, router, down_proj, up_proj, expert_gate, expert_up, expert_down,
    expert_ids, slot_pos, overflow_list,
):
    shards, copies = lax.axis_size("expert"), lax.axis_size("replica")
    columns = shards // CORES
    rows, width = tokens.shape
    latent = down_proj.shape[1]
    bf, f32 = jnp.bfloat16, jnp.float32
    dma = pltpu.SemaphoreType.DMA
    more = max(columns - 1, 1)
    extra = max(copies - 1, 1)
    anywhere, vmem = pl.BlockSpec(memory_space=pl.ANY), pl.BlockSpec(memory_space=pltpu.VMEM)
    return pl.pallas_call(
        functools.partial(layer, shards, copies),
        out_shape=jax.ShapeDtypeStruct((rows, width), bf),
        in_specs=[anywhere, vmem, vmem] + [anywhere] * 5 + [vmem] * 3,
        out_specs=vmem,
        scratch_shapes=[
            pltpu.VMEM((rows, width), bf),
            pltpu.VMEM((rows, width), bf),
            pltpu.VMEM((width, latent), bf),
            pltpu.VMEM((width, latent), bf),
            pltpu.VMEM(expert_gate.shape, bf),
            pltpu.VMEM(expert_up.shape, bf),
            pltpu.VMEM(expert_down.shape, bf),
            pltpu.VMEM((shards, rows, latent), bf),
            pltpu.VMEM((shards, shards, pl.cdiv(expert_gate.shape[0], 8) * 8, rows), f32),
            pltpu.VMEM((rows, expert_gate.shape[2]), bf),
            pltpu.VMEM((rows, latent), f32),
            pltpu.VMEM((rows, latent), f32),
            pltpu.VMEM((shards, rows, latent), bf),
            pltpu.VMEM((shards - 1, rows, latent), bf),
            dma((6,)),
            dma((extra,)), dma((extra,)),
            dma((more, copies)), dma((more, copies)),
            dma((columns,)), dma((columns,)),
            dma((extra, columns)), dma((extra, columns)),
            dma((more,)), dma((more,)),
            dma((columns,)), dma((columns,)),
            dma, dma, dma((more,)), dma((more,)), dma((more,)), dma((more,)),
            dma, dma, dma((more,)), dma((more,)), dma((more,)), dma((more,)),
            dma((shards - 1,)), dma((shards - 1,)),
        ],
        compiler_params=pltpu.CompilerParams(collective_id=0, has_side_effects=True,
                                             vmem_limit_bytes=60 * 1024 * 1024),
    )(
        tokens, norm_gain.reshape(1, -1), router, down_proj, up_proj, expert_gate, expert_up,
        expert_down, expert_ids, slot_pos, overflow_list,
    )


def solution(mesh):
    placed = (
        P(("groups", "expert", "replica"), None),
        P(),
        P(),
        P(("expert", "replica"), None),
        P(("expert", "replica"), None),
        P("expert", None, None),
        P("expert", None, None),
        P("expert", None, None),
        P(("groups", "expert", "replica"), None),
        P(("groups", "expert", "replica"), None),
        P(("groups", "expert", "replica"), None, None, None),
    )
    return jax.shard_map(
        on_device,
        mesh=mesh,
        in_specs=placed,
        out_specs=P(("groups", "expert", "replica"), None),
        check_vma=False,
    )
```

time: 206 us -> 60 us (0.29)
  waiting for transfers between devices: 78.9 us -> 0 us
  local copies, waits for them, and re-layouts: 61.9 us -> 7.1 us
  Pallas kernels: 0 us -> 52.6 us
  matrix products: 24.6 us -> 0 us
  starting transfers between devices: 16.3 us -> 0 us
  between operations: 13.7 us -> 0.01 us
  other arithmetic: 9.75 us -> 0 us
    all_to_all x4 -> x0, waiting for transfers between devices: 54.1 us -> none  [the longest x1 24.7 us: on_device(): lax.all_to_all(outgoing, 'expert', split_axis=1, concat_axis=1, tiled=True)]
    pallas_call x0 -> x1, Pallas kernels: none -> 52.6 us  [on_device(): pl.pallas_call(functools.partial(layer, shards, copies), out_shape=jax.Sh...]
    gather x8 -> x0, local copies, waits for them, and re-layouts: 29.8 us -> none  [the longest x5 17.2 us: on_device(): chosen = jnp.take_along_axis(logits, expert_ids, axis=1)]
    dot_general x5 -> x0, matrix products: 24.6 us -> none  [the longest x1 10.6 us: run_experts(): jnp.einsum('erf,efl->erl', hidden, w_down, preferred_element_type=jnp.flo...]
    all_gather x2 -> x0, waiting for transfers between devices: 23.4 us -> none  [the longest x1 23.4 us: on_device(): lax.all_gather(down_proj, ('expert', 'replica'), axis=0, tiled=True)]
    all_to_all x4 -> x0, starting transfers between devices: 16.3 us -> none  [the longest x1 4.64 us: on_device(): lax.all_to_all(outgoing, 'expert', split_axis=1, concat_axis=1, tiled=True)]
    scatter x1 -> x0, local copies, waits for them, and re-layouts: 11 us -> none  [on_device(): outgoing.at[jnp.where(kept, target, spilled)].set(repeated, mode='drop')]
    slice x5 -> x0, local copies, waits for them, and re-layouts: 6.05 us -> none  [the longest x3 4.53 us: on_device(): done[:, :row_count]]
  transfers between devices with their start and end apart: 6 -> 0, of which waited for: 5 -> 0; matrix products, arithmetic and copies ran while one was open for 36% -> 0% of each run, Pallas kernels for 0% -> 0%
where the time goes in v1:
time: 60 us; the launch traced here: 59.7 us
  Pallas kernels  52.6 us (88%)
  local copies, waits for them, and re-layouts  7.1 us (12%)
    pallas_call x1, Pallas kernels, on_device(): pl.pallas_call(functools.partial(layer, shards, copies), out_shape=jax.Sh...  52.6 us
    unnamed x4, local copies, waits for them, and re-layouts  7.1 us

profile of v1, /device:TPU:0, one launch (start us, length us, event | category | flops | bytes accessed | tf_op | source)
XLA Modules:
  0.0 59.7 jit_solution(12336982906066933015)
XLA Ops:
  0.0 1.5 %copy.13.ids = s32[256,8]{1,0:T(8,128)} copy(s32[256,8]{0,1:T(8,128)} %param.19) | data formatting | bytes 16384 | tf_op args[8]
  1.5 1.5 %copy.14.slot = s32[256,8]{1,0:T(8,128)} copy(s32[256,8]{0,1:T(8,128)} %param.20) | data formatting | bytes 16384 | tf_op args[9]
  3.0 1.8 %copy.12.router = bf16[2048,16]{1,0:T(8,128)(2,1)} copy(bf16[2048,16]{0,1:T(8,128)(2,1)} %param.13) | data formatting | bytes 131072 | tf_op args[2]
  4.8 52.6 %shard_map.109 = bf16[256,2048]{1,0:T(8,128)(2,1)} custom-call(bf16[256,2048]{1,0:T(8,128)(2,1)} %tok.1, f32[1,2048]{1,0:T(1,128)} %bitcast.1, bf16[2048,16]{1,0:T(8,128)(2,1)} %copy.12.router, bf16[128,512]{1,0:T(8,128)(2,1)} %down.1, bf16[128,512]{1,0:T(8,128)(2,1)} %up.1, bf16[4,512,768]{2,1,0:T(8,128)(2,1)} %wg.1, bf16[4,512,768]{2,1,0:T(8,128)(2,1)} %wu.1, ...), custom_call_target="tpu_custom_call" | custom-call | tf_op jit(solution)/shard_map/pallas_call | solution.py:244
  57.4 2.3 %copy.16 = bf16[256,2048]{1,0:T(8,128)(2,1)} copy(bf16[256,2048]{1,0:T(8,128)(2,1)} %shard_map.109) | data formatting | bytes 2097152

commit v2 on v1

--- a/solution.py
+++ b/solution.py
@@ -19,19 +19,19 @@
 
 
 def layer(
-    shards, copies, tok, gain, router, down, up, wg, wu, wd, ids, slot, ov, out,
+    teams, shards, copies, tok, gain, router, down, up, wg, wu, wd, ids, slot, ov, out,
     tokv, normed, dfull, ufull, gv, uv, dv, lat, wts, hid, acc, own, pbuf, rbuf,
     loc, dzs, dzr, dxs, dxr, dcs, dcr, uzs, uzr, uxs, uxr, ucs, ucr,
-    lps, lpr, lxs, lxr, lfs, lfr, wps, wpr, wxs, wxr, wfs, wfr, rs, rr,
+    uys, uyr, lps, lpr, lxs, lxr, lfs, lfr, wps, wpr, wxs, wxr, wfs, wfr, rs, rr,
 ):
     columns = shards // CORES
-    e, r = lax.axis_index("expert"), lax.axis_index("replica")
+    g, e, r = lax.axis_index("groups"), lax.axis_index("expert"), lax.axis_index("replica")
     x, c = e // CORES, e % CORES
     part = rows = down.shape[0]
     local = wg.shape[0]
     tokens = tok.shape[0]
-    top = ids.shape[1]
-    experts = router.shape[1]
+    top = ids.shape[0]
+    experts = router.shape[0]
 
     def ex(xx, cc):
         return xx * CORES + cc
@@ -55,12 +55,26 @@
 
     def at(ref, index, n=1):
         return ref.at[pl.ds(pl.multiple_of(index * part, part), part * n), :]
+
+    def ydev(d):
+        return {"groups": lax.rem(g + d, teams)}
+
+    share = up.shape[1] // teams
+
+    def slab(ref, index, team, n=1):
+        return ref.at[
+            pl.ds(pl.multiple_of(index * part, part), part * n),
+            pl.ds(pl.multiple_of(team * share, share), share),
+        ]
 
     barrier = pltpu.get_barrier_semaphore()
     count = 1
     pl.semaphore_signal(barrier, inc=1, device_id=pdev, device_id_type=MESH)
     for d in range(1, copies):
         pl.semaphore_signal(barrier, inc=1, device_id=zdev(d), device_id_type=MESH)
+        count += 1
+    for d in range(1, teams):
+        pl.semaphore_signal(barrier, inc=1, device_id=ydev(d), device_id_type=MESH)
         count += 1
     for d in range(1, columns):
         for cc in (c, 1 - c):
@@ -71,7 +85,7 @@
     tcopy = pltpu.make_async_copy(tok, tokv, loc.at[0])
     mine = e * copies + r
     dcopy = pltpu.make_async_copy(down, at(dfull, mine), loc.at[1])
-    ucopy = pltpu.make_async_copy(up, at(ufull, mine), loc.at[2])
+    ucopy = pltpu.make_async_copy(slab(up, 0, g), slab(ufull, mine, g), loc.at[2])
     wcopies = [
         pltpu.make_async_copy(wg, gv, loc.at[3]),
         pltpu.make_async_copy(wu, uv, loc.at[4]),
@@ -105,23 +119,23 @@
         scaled = v * lax.rsqrt(jnp.mean(v * v, axis=-1, keepdims=True) + epsilon)
         normed[at_rows, :] = (scaled * gain[...]).astype(jnp.bfloat16)
 
-    logits = jnp.dot(normed[...], router[...], preferred_element_type=jnp.float32)
+    logits = lax.dot_general(
+        router[...], normed[...], (((1,), (1,)), ((), ())), preferred_element_type=jnp.float32
+    )
     sig = 1.0 / (1.0 + jnp.exp(-logits))
-    lane = lax.broadcasted_iota(jnp.int32, (tokens, experts), 1)
-    row = lax.broadcasted_iota(jnp.int32, (tokens, experts), 0)
-    chosen = jnp.zeros((tokens, experts), jnp.float32)
-    served = jnp.zeros((tokens, experts), jnp.float32)
+    expert = lax.broadcasted_iota(jnp.int32, (experts, tokens), 0)
+    first = lax.broadcasted_iota(jnp.int32, (experts, tokens), 1) * top
+    chosen = jnp.zeros((experts, tokens), jnp.float32)
+    served = jnp.zeros((experts, tokens), jnp.float32)
     for k in range(top):
-        hit = lane == ids[:, k : k + 1]
+        hit = expert == ids[k : k + 1, :]
         chosen = jnp.where(hit, 1.0, chosen)
-        served = jnp.where(hit & (slot[:, k : k + 1] >= 0), 1.0, served)
-    listed = jnp.concatenate([ov[0, d] for d in range(shards)], axis=1)
+        served = jnp.where(hit & (slot[k : k + 1, :] >= 0), 1.0, served)
+    listed = jnp.concatenate([ov[0, d] for d in range(shards)], axis=1).T
     for k in range(copies):
-        entry = listed[k : k + 1, :]
-        first = row * top
+        entry = listed[:, k : k + 1]
         served = jnp.where((entry >= first) & (entry < first + top), 1.0, served)
-    weight = served * (sig / jnp.sum(chosen * sig, axis=1, keepdims=True))
-    flipped = weight.T
+    flipped = served * (sig / jnp.sum(chosen * sig, axis=0, keepdims=True))
     wts[e] = jnp.zeros(wts.shape[1:], jnp.float32)
     for d in range(shards):
         wts[e, d, 0:local, :] = flipped[d * local : (d + 1) * local, :]
@@ -135,10 +149,11 @@
     s = e * copies
     go(remote(at(dfull, s, copies), at(dfull, s, copies), dcs.at[0], dcr.at[0], pdev))
     for d in range(1, columns):
-        go(remote(up, at(ufull, mine), uxs.at[d - 1], uxr.at[d - 1], xdev(d)))
+        go(remote(slab(up, 0, g), slab(ufull, mine, g), uxs.at[d - 1], uxr.at[d - 1], xdev(d)))
     ucopy.wait()
     for z in range(1, copies):
-        go(remote(at(ufull, mine), at(ufull, mine), uzs.at[z - 1, 0], uzr.at[z - 1, 0], zdev(z)))
+        here = slab(ufull, mine, g)
+        go(remote(here, here, uzs.at[z - 1, 0], uzr.at[z - 1, 0], zdev(z)))
     for d in range(1, columns):
         base = ex(back(d), c) * copies
         for j in range(copies):
@@ -155,6 +170,21 @@
         go(remote(wts.at[e], wts.at[e], wxs.at[d - 1], wxr.at[d - 1], xdev(d)))
     go(remote(lat.at[e], lat.at[e], lps, lpr, pdev))
     go(remote(wts.at[e], wts.at[e], wps, wpr, pdev))
+
+    for d in range(1, columns):
+        here = slab(ufull, ex(back(d), c) * copies + r, g)
+        remote(here, here, uxs.at[d - 1], uxr.at[d - 1], xdev(d)).wait_recv()
+        for z in range(1, copies):
+            go(remote(here, here, uzs.at[z - 1, d], uzr.at[z - 1, d], zdev(z)))
+
+    def up_across(d):
+        base = ex(back(d), c) * copies
+        for z in range(1, copies):
+            here = slab(ufull, base + zback(z), g)
+            remote(here, here, uzs.at[z - 1, d], uzr.at[z - 1, d], zdev(z)).wait_recv()
+        here = slab(ufull, base, g, copies)
+        for y in range(1, teams):
+            go(remote(here, here, uys.at[y - 1, d], uyr.at[y - 1, d], ydev(y)))
 
     width = wg.shape[2]
     piece = 256
@@ -179,15 +209,11 @@
         w.wait()
     experts_on(e)
     own[...] = acc[...]
-    for d in range(1, columns):
-        s = ex(back(d), c) * copies + r
-        remote(up, at(ufull, s), uxs.at[d - 1], uxr.at[d - 1], xdev(d)).wait_recv()
-        for z in range(1, copies):
-            go(remote(at(ufull, s), at(ufull, s), uzs.at[z - 1, d], uzr.at[z - 1, d], zdev(z)))
     p = ex(x, 1 - c)
     remote(lat.at[p], lat.at[p], lps, lpr, pdev).wait_recv()
     remote(wts.at[p], wts.at[p], wps, wpr, pdev).wait_recv()
     experts_on(p)
+    up_across(0)
     pbuf[p] = acc[...].astype(jnp.bfloat16)
     go(remote(pbuf.at[p], rbuf.at[0], rs.at[0], rr.at[0], pdev))
     for d in range(1, columns):
@@ -205,14 +231,15 @@
         remote(wts.at[q], wts.at[q], wfs.at[d - 1], wfr.at[d - 1], pdev).wait_recv()
         experts_on(q)
         pbuf[q] = acc[...].astype(jnp.bfloat16)
+        up_across(d)
         k = 2 * d
         go(remote(pbuf.at[q], rbuf.at[k], rs.at[k], rr.at[k], {"expert": q}))
 
     for d in range(columns):
         base = ex(back(d), c) * copies
-        for z in range(1, copies):
-            s = base + zback(z)
-            remote(at(ufull, s), at(ufull, s), uzs.at[z - 1, d], uzr.at[z - 1, d], zdev(z)).wait_recv()
+        for y in range(1, teams):
+            here = slab(ufull, base, lax.rem(g - y + teams, teams), copies)
+            remote(here, here, uys.at[y - 1, d], uyr.at[y - 1, d], ydev(y)).wait_recv()
         go(remote(at(ufull, base, copies), at(ufull, base, copies), ucs.at[d], ucr.at[d], pdev))
     for d in range(columns):
         s = ex(back(d), 1 - c) * copies
@@ -233,6 +260,7 @@
     expert_ids, slot_pos, overflow_list,
 ):
     shards, copies = lax.axis_size("expert"), lax.axis_size("replica")
+    teams = lax.axis_size("groups")
     columns = shards // CORES
     rows, width = tokens.shape
     latent = down_proj.shape[1]
@@ -242,7 +270,7 @@
     extra = max(copies - 1, 1)
     anywhere, vmem = pl.BlockSpec(memory_space=pl.ANY), pl.BlockSpec(memory_space=pltpu.VMEM)
     return pl.pallas_call(
-        functools.partial(layer, shards, copies),
+        functools.partial(layer, teams, shards, copies),
         out_shape=jax.ShapeDtypeStruct((rows, width), bf),
         in_specs=[anywhere, vmem, vmem] + [anywhere] * 5 + [vmem] * 3,
         out_specs=vmem,
@@ -268,6 +296,7 @@
             dma((extra, columns)), dma((extra, columns)),
             dma((more,)), dma((more,)),
             dma((columns,)), dma((columns,)),
+            dma((max(teams - 1, 1), columns)), dma((max(teams - 1, 1), columns)),
             dma, dma, dma((more,)), dma((more,)), dma((more,)), dma((more,)),
             dma, dma, dma((more,)), dma((more,)), dma((more,)), dma((more,)),
             dma((shards - 1,)), dma((shards - 1,)),
@@ -275,8 +304,8 @@
         compiler_params=pltpu.CompilerParams(collective_id=0, has_side_effects=True,
                                              vmem_limit_bytes=60 * 1024 * 1024),
     )(
-        tokens, norm_gain.reshape(1, -1), router, down_proj, up_proj, expert_gate, expert_up,
-        expert_down, expert_ids, slot_pos, overflow_list,
+        tokens, norm_gain.reshape(1, -1), router.T, down_proj, up_proj, expert_gate, expert_up,
+        expert_down, expert_ids.T, slot_pos.T, overflow_list,
     )
 
 

time: 60 us -> 53.9 us (0.90)
  local copies, waits for them, and re-layouts: 7.1 us -> 2.3 us
  Pallas kernels: 52.6 us -> 51.4 us
    unnamed x4 -> x1, local copies, waits for them, and re-layouts: 7.1 us -> 2.3 us
    pallas_call x1, Pallas kernels: 52.6 us -> 51.4 us  [on_device(): pl.pallas_call(functools.partial(layer, teams, shards, copies), out_shape...]
where the time goes in v2:
time: 53.9 us; the launch traced here: 53.7 us
  Pallas kernels  51.4 us (95%)
  local copies, waits for them, and re-layouts  2.3 us (4%)
    pallas_call x1, Pallas kernels, on_device(): pl.pallas_call(functools.partial(layer, teams, shards, copies), out_shape...  51.4 us
    unnamed x1, local copies, waits for them, and re-layouts  2.3 us

profile of v2, /device:TPU:0, one launch (start us, length us, event | category | flops | bytes accessed | tf_op | source)
XLA Modules:
  0.0 53.7 jit_solution(5549833750205701689)
XLA Ops:
  0.0 51.4 %shard_map.109 = bf16[256,2048]{1,0:T(8,128)(2,1)} custom-call(bf16[256,2048]{1,0:T(8,128)(2,1)} %tok.1, f32[1,2048]{1,0:T(1,128)} %bitcast.5, bf16[16,2048]{1,0:T(8,128)(2,1)} %bitcast.4, bf16[128,512]{1,0:T(8,128)(2,1)} %down.1, bf16[128,512]{1,0:T(8,128)(2,1)} %up.1, bf16[4,512,768]{2,1,0:T(8,128)(2,1)} %wg.1, bf16[4,512,768]{2,1,0:T(8,128)(2,1)} %wu.1, ...), custom_call_target="tpu_custom_call" | custom-call | tf_op jit(solution)/shard_map/pallas_call | solution.py:272
  51.4 2.3 %copy.13 = bf16[256,2048]{1,0:T(8,128)(2,1)} copy(bf16[256,2048]{1,0:T(8,128)(2,1)} %shard_map.109) | data formatting | bytes 2097152

commit v3 on v2

--- a/solution.py
+++ b/solution.py
@@ -21,8 +21,9 @@
 def layer(
     teams, shards, copies, tok, gain, router, down, up, wg, wu, wd, ids, slot, ov, out,
     tokv, normed, dfull, ufull, gv, uv, dv, lat, wts, hid, acc, own, pbuf, rbuf,
-    loc, dzs, dzr, dxs, dxr, dcs, dcr, uzs, uzr, uxs, uxr, ucs, ucr,
-    uys, uyr, lps, lpr, lxs, lxr, lfs, lfr, wps, wpr, wxs, wxr, wfs, wfr, rs, rr,
+    rows_in, gate, far, stage,
+    loc, dzs, dzr, dxs, dxr, dcs, dcr, dys, dyr, uzs, uzr, uxs, uxr, ucs, ucr, uys, uyr,
+    lps, lpr, lxs, lxr, lfs, lfr, wps, wpr, wxs, wxr, wfs, wfr, rs, rr, sts, str_,
 ):
     columns = shards // CORES
     g, e, r = lax.axis_index("groups"), lax.axis_index("expert"), lax.axis_index("replica")
@@ -60,6 +61,15 @@
         return {"groups": lax.rem(g + d, teams)}
 
     share = up.shape[1] // teams
+
+    lent = part * 3 // 8 // 16 * 16 if teams == 2 else 0
+    kept = part - lent
+
+    def fetched(ref, index):
+        return ref.at[pl.ds(pl.multiple_of(index * part + g * lent, 16), kept), :]
+
+    def swapped(index, team):
+        return dfull.at[pl.ds(pl.multiple_of(index * part + team * kept, 16), lent), :]
 
     def slab(ref, index, team, n=1):
         return ref.at[
@@ -102,9 +112,10 @@
         sends.append(copy)
 
     for d in range(1, columns):
-        go(remote(down, at(dfull, mine), dxs.at[d - 1, 0], dxr.at[d - 1, 0], xdev(d)))
+        go(remote(fetched(down, 0), fetched(dfull, mine), dxs.at[d - 1, 0], dxr.at[d - 1, 0], xdev(d)))
     for d in range(1, copies):
-        go(remote(down, at(dfull, mine), dzs.at[d - 1], dzr.at[d - 1], zdev(d)))
+        go(remote(fetched(down, 0), fetched(dfull, mine), dzs.at[d - 1], dzr.at[d - 1], zdev(d)))
+    go(remote(down, at(dfull, mine), dcs.at[0, 0, 0], dcr.at[0, 0, 0], pdev))
     ucopy.start()
     for w in wcopies:
         w.start()
@@ -140,36 +151,69 @@
     for d in range(shards):
         wts[e, d, 0:local, :] = flipped[d * local : (d + 1) * local, :]
 
+    def down_on(d, j):
+        s = ex(back(d), c) * copies + zback(j)
+        here = fetched(dfull, s)
+        go(remote(here, here, dcs.at[d, j, 0], dcr.at[d, j, 0], pdev))
+        if lent:
+            here = swapped(s, g)
+            go(remote(here, here, dys.at[d, j], dyr.at[d, j], ydev(1)))
+
+    def down_z(j):
+        here = fetched(dfull, e * copies + zback(j))
+        remote(here, here, dzs.at[j - 1], dzr.at[j - 1], zdev(j)).wait_recv()
+        for d in range(1, columns):
+            go(remote(here, here, dxs.at[d - 1, j], dxr.at[d - 1, j], xdev(d)))
+        down_on(0, j)
+
+    def down_x(j):
+        for d in range(1, columns):
+            here = fetched(dfull, ex(back(d), c) * copies + zback(j))
+            remote(here, here, dxs.at[d - 1, j], dxr.at[d - 1, j], xdev(d)).wait_recv()
+            down_on(d, j)
+
     for j in range(1, copies):
-        s = e * copies + zback(j)
-        remote(down, at(dfull, s), dzs.at[j - 1], dzr.at[j - 1], zdev(j)).wait_recv()
-        for d in range(1, columns):
-            go(remote(at(dfull, s), at(dfull, s), dxs.at[d - 1, j], dxr.at[d - 1, j], xdev(d)))
-    dcopy.wait()
-    s = e * copies
-    go(remote(at(dfull, s, copies), at(dfull, s, copies), dcs.at[0], dcr.at[0], pdev))
+        down_z(j)
+        down_x(j - 1)
     for d in range(1, columns):
         go(remote(slab(up, 0, g), slab(ufull, mine, g), uxs.at[d - 1], uxr.at[d - 1], xdev(d)))
     ucopy.wait()
     for z in range(1, copies):
         here = slab(ufull, mine, g)
         go(remote(here, here, uzs.at[z - 1, 0], uzr.at[z - 1, 0], zdev(z)))
-    for d in range(1, columns):
-        base = ex(back(d), c) * copies
-        for j in range(copies):
-            s = base + zback(j)
-            remote(at(dfull, s), at(dfull, s), dxs.at[d - 1, j], dxr.at[d - 1, j], xdev(d)).wait_recv()
-        go(remote(at(dfull, base, copies), at(dfull, base, copies), dcs.at[d], dcr.at[d], pdev))
-    for d in range(columns):
-        s = ex(back(d), 1 - c) * copies
-        remote(at(dfull, s, copies), at(dfull, s, copies), dcs.at[d], dcr.at[d], pdev).wait_recv()
+    down_x(copies - 1)
+    others = [(d, j) for d in range(columns) for j in range(copies) if d + j]
+    if lent:
+        for d, j in others:
+            here = swapped(ex(back(d), c) * copies + zback(j), 1 - g)
+            remote(here, here, dys.at[d, j], dyr.at[d, j], ydev(1)).wait_recv()
+            go(remote(here, here, dcs.at[d, j, 1], dcr.at[d, j, 1], pdev))
+    dcopy.wait()
+    here = at(dfull, ex(x, 1 - c) * copies + r)
+    remote(here, here, dcs.at[0, 0, 0], dcr.at[0, 0, 0], pdev).wait_recv()
+    for d, j in others:
+        s = ex(back(d), 1 - c) * copies + zback(j)
+        here = fetched(dfull, s)
+        remote(here, here, dcs.at[d, j, 0], dcr.at[d, j, 0], pdev).wait_recv()
+        if lent:
+            here = swapped(s, 1 - g)
+            remote(here, here, dcs.at[d, j, 1], dcr.at[d, j, 1], pdev).wait_recv()
 
     lat[e] = jnp.dot(normed[...], dfull[...], preferred_element_type=jnp.float32).astype(jnp.bfloat16)
-    for d in range(1, columns):
-        go(remote(lat.at[e], lat.at[e], lxs.at[d - 1], lxr.at[d - 1], xdev(d)))
+    half = tokens // 2
+
+    def half_of(ref, index, h):
+        return ref.at[index, pl.ds(h * half, half), :]
+
+    for d in range(1, columns):
         go(remote(wts.at[e], wts.at[e], wxs.at[d - 1], wxr.at[d - 1], xdev(d)))
+        here = half_of(lat, e, 0)
+        go(remote(here, here, lxs.at[d - 1, 0], lxr.at[d - 1, 0], xdev(d)))
+    go(remote(wts.at[e], wts.at[e], wps, wpr, pdev))
     go(remote(lat.at[e], lat.at[e], lps, lpr, pdev))
-    go(remote(wts.at[e], wts.at[e], wps, wpr, pdev))
+    for d in range(1, columns):
+        here = half_of(lat, e, 1)
+        go(remote(here, here, lxs.at[d - 1, 1], lxr.at[d - 1, 1], xdev(d)))
 
     for d in range(1, columns):
         here = slab(ufull, ex(back(d), c) * copies + r, g)
@@ -189,51 +233,80 @@
     width = wg.shape[2]
     piece = 256
 
-    def experts_on(which):
-        scale = wts[which, e].T
-        spot = lax.broadcasted_iota(jnp.int32, scale.shape, 1)
+    def experts_on(pieces, middle):
+        block = [lat[which, lo : lo + n, :] for which, lo, n in pieces]
+        rows_in[...] = block[0] if len(block) == 1 else jnp.concatenate(block, axis=0)
+        scale = [wts[which, e].T[lo : lo + n] for which, lo, n in pieces]
+        gate[...] = scale[0] if len(scale) == 1 else jnp.concatenate(scale, axis=0)
         acc[...] = jnp.zeros_like(acc)
 
-        @pl.loop(0, local)
-        def _(n):
-            block = lat[which]
-            weights = jnp.sum(jnp.where(spot == n, scale, 0.0), axis=1, keepdims=True)
+        def one(n):
+            inner = rows_in[...]
+            spot = lax.broadcasted_iota(jnp.int32, gate.shape, 1)
+            weights = jnp.sum(jnp.where(spot == n, gate[...], 0.0), axis=1, keepdims=True)
             for f in range(0, width, piece):
-                a = jnp.dot(block, gv[n, :, f : f + piece], preferred_element_type=jnp.float32)
-                b = jnp.dot(block, uv[n, :, f : f + piece], preferred_element_type=jnp.float32)
+                a = jnp.dot(inner, gv[n, :, f : f + piece], preferred_element_type=jnp.float32)
+                b = jnp.dot(inner, uv[n, :, f : f + piece], preferred_element_type=jnp.float32)
                 h = a / (1.0 + jnp.exp(-a)) * b * weights
                 hid[:, f : f + piece] = h.astype(jnp.bfloat16)
             acc[...] += jnp.dot(hid[...], dv[n], preferred_element_type=jnp.float32)
 
+        pl.loop(0, local // 2)(one)
+        middle()
+        pl.loop(local // 2, local)(one)
+
+    def pass_on(h):
+        for d in range(1, columns):
+            q = ex(back(d), c)
+            if h == 0:
+                remote(wts.at[q], wts.at[q], wxs.at[d - 1], wxr.at[d - 1], xdev(d)).wait_recv()
+                go(remote(wts.at[q], wts.at[q], wfs.at[d - 1], wfr.at[d - 1], pdev))
+            here = half_of(lat, q, h)
+            remote(here, here, lxs.at[d - 1, h], lxr.at[d - 1, h], xdev(d)).wait_recv()
+            go(remote(here, here, lfs.at[d - 1, h], lfr.at[d - 1, h], pdev))
+
     for w in wcopies:
         w.wait()
-    experts_on(e)
+    experts_on([(e, 0, tokens)], lambda: None)
     own[...] = acc[...]
     p = ex(x, 1 - c)
+    remote(wts.at[p], wts.at[p], wps, wpr, pdev).wait_recv()
     remote(lat.at[p], lat.at[p], lps, lpr, pdev).wait_recv()
-    remote(wts.at[p], wts.at[p], wps, wpr, pdev).wait_recv()
-    experts_on(p)
+    experts_on([(p, 0, tokens)], lambda: pass_on(0))
+    pbuf[p] = acc[...].astype(jnp.bfloat16)
+    go(remote(pbuf.at[p], rbuf.at[0], rs.at[0, 0], rr.at[0, 0], pdev))
     up_across(0)
-    pbuf[p] = acc[...].astype(jnp.bfloat16)
-    go(remote(pbuf.at[p], rbuf.at[0], rs.at[0], rr.at[0], pdev))
-    for d in range(1, columns):
+
+    def settle(d, h):
+        span = slice(h * half, (h + 1) * half)
         q = ex(back(d), c)
-        remote(lat.at[q], lat.at[q], lxs.at[d - 1], lxr.at[d - 1], xdev(d)).wait_recv()
-        remote(wts.at[q], wts.at[q], wxs.at[d - 1], wxr.at[d - 1], xdev(d)).wait_recv()
-        go(remote(lat.at[q], lat.at[q], lfs.at[d - 1], lfr.at[d - 1], pdev))
-        go(remote(wts.at[q], wts.at[q], wfs.at[d - 1], wfr.at[d - 1], pdev))
-        experts_on(q)
-        pbuf[q] = acc[...].astype(jnp.bfloat16)
-        k = 2 * d - 1
-        go(remote(pbuf.at[q], rbuf.at[k], rs.at[k], rr.at[k], {"expert": q}))
-        q = ex(back(d), 1 - c)
-        remote(lat.at[q], lat.at[q], lfs.at[d - 1], lfr.at[d - 1], pdev).wait_recv()
-        remote(wts.at[q], wts.at[q], wfs.at[d - 1], wfr.at[d - 1], pdev).wait_recv()
-        experts_on(q)
-        pbuf[q] = acc[...].astype(jnp.bfloat16)
-        up_across(d)
-        k = 2 * d
-        go(remote(pbuf.at[q], rbuf.at[k], rs.at[k], rr.at[k], {"expert": q}))
+        here = half_of(stage, d - 1, h)
+        remote(here, here, sts.at[d - 1, h], str_.at[d - 1, h], pdev).wait_recv()
+        total = far[h] + stage[d - 1, span, :].astype(jnp.float32)
+        pbuf[q, span, :] = total.astype(jnp.bfloat16)
+        go(remote(half_of(pbuf, q, h), half_of(rbuf, d, h), rs.at[d, h], rr.at[d, h], {"expert": q}))
+
+    for d in range(1, columns):
+        q, t = ex(back(d), c), ex(back(d), 1 - c)
+        for h in range(2):
+            if h == 0:
+                remote(wts.at[t], wts.at[t], wfs.at[d - 1], wfr.at[d - 1], pdev).wait_recv()
+            here = half_of(lat, t, h)
+            remote(here, here, lfs.at[d - 1, h], lfr.at[d - 1, h], pdev).wait_recv()
+
+            def middle():
+                if h == 0 and d == 1:
+                    pass_on(1)
+                if h == 1:
+                    settle(d, 0)
+                    up_across(d)
+
+            experts_on([(t, h * half, half), (q, h * half, half)], middle)
+            pbuf[t, h * half : (h + 1) * half, :] = acc[0:half, :].astype(jnp.bfloat16)
+            go(remote(half_of(pbuf, t, h), half_of(stage, d - 1, h), sts.at[d - 1, h],
+                      str_.at[d - 1, h], pdev))
+            far[h] = acc[half:, :]
+        settle(d, 1)
 
     for d in range(columns):
         base = ex(back(d), c) * copies
@@ -244,13 +317,18 @@
     for d in range(columns):
         s = ex(back(d), 1 - c) * copies
         remote(at(ufull, s, copies), at(ufull, s, copies), ucs.at[d], ucr.at[d], pdev).wait_recv()
-    for k in range(shards - 1):
-        remote(rbuf.at[k], rbuf.at[k], rs.at[k], rr.at[k], pdev).wait_recv()
-        own[...] += rbuf[k].astype(jnp.float32)
-    out[...] = lax.dot_general(
-        own[...].astype(jnp.bfloat16), ufull[...], (((1,), (1,)), ((), ())),
-        preferred_element_type=jnp.float32,
-    ).astype(jnp.bfloat16)
+    remote(rbuf.at[0], rbuf.at[0], rs.at[0, 0], rr.at[0, 0], pdev).wait_recv()
+    for h in range(2):
+        span = slice(h * half, (h + 1) * half)
+        total = own[span, :] + rbuf[0, span, :].astype(jnp.float32)
+        for d in range(1, columns):
+            here = half_of(rbuf, d, h)
+            remote(here, here, rs.at[d, h], rr.at[d, h], xdev(d)).wait_recv()
+            total = total + rbuf[d, span, :].astype(jnp.float32)
+        out[span, :] = lax.dot_general(
+            total.astype(jnp.bfloat16), ufull[...], (((1,), (1,)), ((), ())),
+            preferred_element_type=jnp.float32,
+        ).astype(jnp.bfloat16)
     for copy in sends:
         copy.wait_send()
 
@@ -288,18 +366,23 @@
             pltpu.VMEM((rows, latent), f32),
             pltpu.VMEM((rows, latent), f32),
             pltpu.VMEM((shards, rows, latent), bf),
-            pltpu.VMEM((shards - 1, rows, latent), bf),
+            pltpu.VMEM((columns, rows, latent), bf),
+            pltpu.VMEM((rows, latent), bf),
+            pltpu.VMEM((rows, pl.cdiv(expert_gate.shape[0], 8) * 8), f32),
+            pltpu.VMEM((2, rows // 2, latent), f32),
+            pltpu.VMEM((more, rows, latent), bf),
             dma((6,)),
             dma((extra,)), dma((extra,)),
             dma((more, copies)), dma((more, copies)),
-            dma((columns,)), dma((columns,)),
+            dma((columns, copies, 2)), dma((columns, copies, 2)),
+            dma((columns, copies)), dma((columns, copies)),
             dma((extra, columns)), dma((extra, columns)),
             dma((more,)), dma((more,)),
             dma((columns,)), dma((columns,)),
             dma((max(teams - 1, 1), columns)), dma((max(teams - 1, 1), columns)),
+            dma, dma, dma((more, 2)), dma((more, 2)), dma((more, 2)), dma((more, 2)),
             dma, dma, dma((more,)), dma((more,)), dma((more,)), dma((more,)),
-            dma, dma, dma((more,)), dma((more,)), dma((more,)), dma((more,)),
-            dma((shards - 1,)), dma((shards - 1,)),
+            dma((columns, 2)), dma((columns, 2)), dma((more, 2)), dma((more, 2)),
         ],
         compiler_params=pltpu.CompilerParams(collective_id=0, has_side_effects=True,
                                              vmem_limit_bytes=60 * 1024 * 1024),

time: 53.9 us -> 51.3 us (0.952)
  Pallas kernels: 51.4 us -> 48.8 us
    pallas_call x1, Pallas kernels: 51.4 us -> 48.8 us  [on_device(): pl.pallas_call(functools.partial(layer, teams, shards, copies), out_shape...]
where the time goes in v3:
time: 51.3 us; the launch traced here: 51.1 us
  Pallas kernels  48.8 us (95%)
  local copies, waits for them, and re-layouts  2.3 us (4%)
    pallas_call x1, Pallas kernels, on_device(): pl.pallas_call(functools.partial(layer, teams, shards, copies), out_shape...  48.8 us
    unnamed x1, local copies, waits for them, and re-layouts  2.3 us

profile of v3, /device:TPU:0, one launch (start us, length us, event | category | flops | bytes accessed | tf_op | source)
XLA Modules:
  0.0 51.1 jit_solution(2141615696812358069)
XLA Ops:
  0.0 48.8 %shard_map.109 = bf16[256,2048]{1,0:T(8,128)(2,1)} custom-call(bf16[256,2048]{1,0:T(8,128)(2,1)} %tok.1, f32[1,2048]{1,0:T(1,128)} %bitcast.5, bf16[16,2048]{1,0:T(8,128)(2,1)} %bitcast.4, bf16[128,512]{1,0:T(8,128)(2,1)} %down.1, bf16[128,512]{1,0:T(8,128)(2,1)} %up.1, bf16[4,512,768]{2,1,0:T(8,128)(2,1)} %wg.1, bf16[4,512,768]{2,1,0:T(8,128)(2,1)} %wu.1, ...), custom_call_target="tpu_custom_call" | custom-call | tf_op jit(solution)/shard_map/pallas_call | solution.py:350
  48.8 2.3 %copy.13 = bf16[256,2048]{1,0:T(8,128)(2,1)} copy(bf16[256,2048]{1,0:T(8,128)(2,1)} %shard_map.109) | data formatting | bytes 2097152

commit v4 on v3

--- a/solution.py
+++ b/solution.py
@@ -62,7 +62,7 @@
 
     share = up.shape[1] // teams
 
-    lent = part * 3 // 8 // 16 * 16 if teams == 2 else 0
+    lent = part // 2 // 16 * 16 if teams == 2 else 0
     kept = part - lent
 
     def fetched(ref, index):
@@ -150,6 +150,10 @@
     wts[e] = jnp.zeros(wts.shape[1:], jnp.float32)
     for d in range(shards):
         wts[e, d, 0:local, :] = flipped[d * local : (d + 1) * local, :]
+
+    for d in range(1, columns):
+        go(remote(wts.at[e], wts.at[e], wxs.at[d - 1], wxr.at[d - 1], xdev(d)))
+    go(remote(wts.at[e], wts.at[e], wps, wpr, pdev))
 
     def down_on(d, j):
         s = ex(back(d), c) * copies + zback(j)
@@ -199,21 +203,20 @@
             here = swapped(s, 1 - g)
             remote(here, here, dcs.at[d, j, 1], dcr.at[d, j, 1], pdev).wait_recv()
 
-    lat[e] = jnp.dot(normed[...], dfull[...], preferred_element_type=jnp.float32).astype(jnp.bfloat16)
     half = tokens // 2
 
     def half_of(ref, index, h):
         return ref.at[index, pl.ds(h * half, half), :]
 
-    for d in range(1, columns):
-        go(remote(wts.at[e], wts.at[e], wxs.at[d - 1], wxr.at[d - 1], xdev(d)))
-        here = half_of(lat, e, 0)
-        go(remote(here, here, lxs.at[d - 1, 0], lxr.at[d - 1, 0], xdev(d)))
-    go(remote(wts.at[e], wts.at[e], wps, wpr, pdev))
+    for h in range(2):
+        span = slice(h * half, (h + 1) * half)
+        lat[e, span, :] = jnp.dot(
+            normed[span, :], dfull[...], preferred_element_type=jnp.float32
+        ).astype(jnp.bfloat16)
+        for d in range(1, columns):
+            here = half_of(lat, e, h)
+            go(remote(here, here, lxs.at[d - 1, h], lxr.at[d - 1, h], xdev(d)))
     go(remote(lat.at[e], lat.at[e], lps, lpr, pdev))
-    for d in range(1, columns):
-        here = half_of(lat, e, 1)
-        go(remote(here, here, lxs.at[d - 1, 1], lxr.at[d - 1, 1], xdev(d)))
 
     for d in range(1, columns):
         here = slab(ufull, ex(back(d), c) * copies + r, g)

time: 51.3 us -> 50.8 us (level)
    pallas_call x1, Pallas kernels: 48.8 us -> 48.3 us  [on_device(): pl.pallas_call(functools.partial(layer, teams, shards, copies), out_shape...]
where the time goes in v4:
time: 50.8 us; the launch traced here: 50.6 us
  Pallas kernels  48.3 us (95%)
  local copies, waits for them, and re-layouts  2.3 us (5%)
    pallas_call x1, Pallas kernels, on_device(): pl.pallas_call(functools.partial(layer, teams, shards, copies), out_shape...  48.3 us
    unnamed x1, local copies, waits for them, and re-layouts  2.3 us

profile of v4, /device:TPU:0, one launch (start us, length us, event | category | flops | bytes accessed | tf_op | source)
XLA Modules:
  0.0 50.6 jit_solution(5728794286372827060)
XLA Ops:
  0.0 48.3 %shard_map.109 = bf16[256,2048]{1,0:T(8,128)(2,1)} custom-call(bf16[256,2048]{1,0:T(8,128)(2,1)} %tok.1, f32[1,2048]{1,0:T(1,128)} %bitcast.5, bf16[16,2048]{1,0:T(8,128)(2,1)} %bitcast.4, bf16[128,512]{1,0:T(8,128)(2,1)} %down.1, bf16[128,512]{1,0:T(8,128)(2,1)} %up.1, bf16[4,512,768]{2,1,0:T(8,128)(2,1)} %wg.1, bf16[4,512,768]{2,1,0:T(8,128)(2,1)} %wu.1, ...), custom_call_target="tpu_custom_call" | custom-call | tf_op jit(solution)/shard_map/pallas_call | solution.py:353
  48.3 2.3 %copy.13 = bf16[256,2048]{1,0:T(8,128)(2,1)} copy(bf16[256,2048]{1,0:T(8,128)(2,1)} %shard_map.109) | data formatting | bytes 2097152
